TPU v7x, 32 devices: a whole 2x2x4 slice. The times are simulated.
32 devices in a mesh: prow: 4 (over y, x), pcol: 8 (over z, core).
Axes of the slice: x: 2, y: 2, z: 4, core: 2. Of those that a mesh axis runs over, the one named last changes fastest.
Arguments:
- anc_inverse: bfloat16 [6, 1024, 3, 2048], P(None, 'prow', None, 'pcol'), may hold values from -0.078125 to 0.078125
- panel: bfloat16 [3, 6, 4, 256, 512], P(None, None, 'prow', 'pcol'), may hold values from -1.1953125 to 1.1953125
- tile_mask: int32 [3, 24], replicated, may hold values 0 or 1
- diag_inverse: float32 [3, 512, 512], P(None, ('prow', 'pcol')), may hold values from -6 to 6
Outputs:
- block_column: bfloat16 [3, 6, 4, 256, 512], P(None, None, 'prow', 'pcol')
- diag_block: float32 [3, 512, 512], P(None, ('prow', 'pcol'))
All inputs are finite; a program needn't handle non-finite values.
Results may differ from a plain program's by a relative error of at most 0.0017.
Values may be sent and summed in bfloat16 or wider, within the bound.
No kernel may reach another device: no remote copies, remote signals or barrier semaphores. Data moves between devices by JAX's collectives and lax.ppermute only.
A program may use at most 128 MiB of HBM per device.

v0:
```python
import jax
import jax.numpy as jnp
from jax import lax
from jax.sharding import PartitionSpec as P


def spread(x, axis, root):
    mine = lax.axis_index(axis) == root
    return lax.psum(jnp.where(mine, x, jnp.zeros_like(x)), axis)


def local_product(anc_block, columns):
    return jnp.einsum("aibj,sbjw->isaw", anc_block, columns, preferred_element_type=jnp.float32)


def outbound(masked, n_row, n_col):
    groups, tile_rows, single, sub_rows, width = masked.shape
    tile_cols = tile_rows * n_row // n_col
    grouped = masked.reshape(groups, tile_cols, n_col // n_row, sub_rows, width)
    return jnp.repeat(grouped, n_row, axis=2)


def body(anc_inverse, panel, tile_mask, diag_inverse):
    n_row = lax.axis_size("prow")
    n_col = lax.axis_size("pcol")
    row_pos = lax.axis_index("prow")
    col_pos = lax.axis_index("pcol")
    sets, tile_rows, single, sub_rows, width = panel.shape
    tiles = tile_mask.shape[1]
    tile_size = anc_inverse.shape[1]
    row_ids = jnp.arange(tile_rows, dtype=jnp.int32) * n_row + row_pos
    hits = (row_ids[:, None] == jnp.arange(tiles, dtype=jnp.int32)[None, :]).astype(jnp.int32)
    row_mask = jnp.sum(tile_mask[:, None, :] * hits[None], axis=2)
    keep = row_mask.astype(jnp.bfloat16)[:, :, None, None, None]
    masked = panel * keep
    outgoing = outbound(masked, n_row, n_col)
    root = col_pos % n_row
    arrived = lax.all_to_all(outgoing, "pcol", split_axis=2, concat_axis=3, tiled=True)
    columns = spread(arrived.reshape(sets, -1, tile_size, width), "prow", root)
    summed = lax.psum_scatter(
        local_product(anc_inverse, columns), "pcol", scatter_dimension=0, tiled=True
    )
    image = -jnp.transpose(summed, (1, 2, 0, 3))[:, :, None] * keep.astype(jnp.float32)
    block_column = image.astype(jnp.bfloat16)
    partial_value = jnp.einsum(
        "saxiw,saxiv->swv", masked, block_column, preferred_element_type=jnp.float32
    )
    mine = lax.psum_scatter(partial_value, ("prow", "pcol"), scatter_dimension=1, tiled=True)
    diag_block = diag_inverse - mine
    return (block_column, diag_block)


def solution(mesh):
    in_specs = (
        P(None, "prow", None, "pcol"),
        P(None, None, "prow", "pcol", None),
        P(),
        P(None, ("prow", "pcol"), None),
    )
    out_specs = (P(None, None, "prow", "pcol", None), P(None, ("prow", "pcol"), None))
    return jax.shard_map(body, mesh=mesh, in_specs=in_specs, out_specs=out_specs, check_vma=False)
```

profile of v0, /device:TPU:0, one launch (start us, length us, event | category | flops | bytes accessed | tf_op | source)
XLA Modules:
  0.0 455.2 jit_solution(3141937686562053441)
XLA Ops:
  7.2 0.0 copy-start
  7.2 0.1 fusion.6
  7.3 1.0 multiply_reduce_fusion
  8.2 1.2 broadcast_multiply_fusion
  9.4 0.0 copy-start.1
  9.4 0.8 copy-done.1
  10.3 1.7 broadcast_in_dim.4
  12.0 6.4 %all-to-all-start = ((bf16[3,3,8,32,512]{4,3,1,0,2:T(8,128)(2,1)}), bf16[3,3,8,32,512]{4,3,1,0,2:T(8,128)(2,1)}, u32[]{:S(2)}, u32[]{:S(2)}) async-start(bf16[3,3,8,32,512]{4,3,1,0,2:T(8,128)(2,1)} %bitcast.27), calls=%async_computation | async-start | bytes 4718592 | tf_op jit(solution)/shard_map/all_to_all | solution.py:38
  18.4 0.0 all-reduce.2.cloned.1.call-start
  18.4 54.7 %all-to-all-done = bf16[3,3,8,32,512]{4,3,1,0,2:T(8,128)(2,1)} async-done(((bf16[3,3,8,32,512]{4,3,1,0,2:T(8,128)(2,1)}), bf16[3,3,8,32,512]{4,3,1,0,2:T(8,128)(2,1)}, u32[]{:S(2)}, u32[]{:S(2)}) %all-to-all-start) | async-done | bytes 2359328 | tf_op jit(solution)/shard_map/all_to_all | solution.py:38
  73.1 3.2 copy_select_fusion
  76.3 4.3 copy.20
  80.6 0.0 all-reduce.2.cloned.1.call-update
  80.6 0.0 reduce-scatter.3.cloned.1.call-start
  80.7 72.9 %all-reduce.2.cloned.1.call-done = bf16[3,3,256,512]{2,3,1,0:T(8,128)(2,1)} async-done(((bf16[3,3,256,512]{2,3,1,0:T(8,128)(2,1)}), bf16[3,3,256,512]{2,3,1,0:T(8,128)(2,1)}) %all-reduce.2.cloned.1.call-update) | async-done | bytes 2359312 | tf_op jit(solution)/shard_map/psum | solution.py:9
  153.6 0.0 copy-done
  153.6 7.9 %convolution_bitcast_fusion = f32[256,3,6,512]{0,3,2,1:T(8,128)} fusion(bf16[3,3,256,512]{2,3,1,0:T(8,128)(2,1)} %all-reduce.2.cloned.1.call-done, bf16[6,256,3,256]{3,1,2,0:T(8,128)(2,1)S(1)} %copy-done), kind=kOutput, calls=%fused_computation | convolution fusion | flops 3623878656 | bytes 14155776 | tf_op jit(solution)/shard_map/aibj,sbjw->isaw/dot_general | solution.py:13
  161.5 11.9 %copy.21 = f32[256,3,6,512]{3,2,1,0:T(8,128)} copy(f32[256,3,6,512]{0,3,2,1:T(8,128)} %convolution_bitcast_fusion) | data formatting | bytes 18874368 | tf_op jit(solution)/shard_map/aibj,sbjw->isaw/transpose | solution.py:13
  173.4 0.0 reduce-scatter.3.cloned.1.call-update
  173.4 0.0 reduce-scatter.5.cloned.1.call-start
  173.4 129.2 %reduce-scatter.3.cloned.1.call-done = f32[32,3,6,512]{3,2,1,0:T(8,128)} async-done(((f32[256,3,6,512]{3,2,1,0:T(8,128)}), f32[32,3,6,512]{3,2,1,0:T(8,128)}) %reduce-scatter.3.cloned.1.call-update) | async-done | bytes 1179664 | tf_op jit(solution)/shard_map/reduce_scatter | solution.py:40
  302.7 1.8 fusion.5
  304.4 3.4 convolution_bitcast_fusion.1
  307.8 0.0 copy-start.2
  307.8 0.0 reduce-scatter.5.cloned.1.call-update
  307.8 1.0 copy.23
  308.8 138.3 %reduce-scatter.5.cloned.1.call-done = f32[3,16,512]{2,1,0:T(8,128)} async-done(((f32[3,512,512]{2,1,0:T(8,128)}), f32[3,16,512]{2,1,0:T(8,128)}) %reduce-scatter.5.cloned.1.call-update) | async-done | bytes 98320 | tf_op jit(solution)/shard_map/reduce_scatter | solution.py:48
  447.1 0.0 copy-done.2
  447.1 1.5 sub.3
  (3 shorter events, 0.1 us)
Async XLA Ops:
  7.2 146.4 %copy-start = (bf16[6,256,3,256]{3,1,2,0:T(8,128)(2,1)S(1)}, bf16[6,256,3,256]{3,1,2,0:T(8,128)(2,1)}, u32[]{:S(2)}) copy-start(bf16[6,256,3,256]{3,1,2,0:T(8,128)(2,1)} %param.4) | copy-start | bytes 7077892
  9.4 0.8 copy-start.1
  12.0 61.1 %all-to-all-start = ((bf16[3,3,8,32,512]{4,3,1,0,2:T(8,128)(2,1)}), bf16[3,3,8,32,512]{4,3,1,0,2:T(8,128)(2,1)}, u32[]{:S(2)}, u32[]{:S(2)}) async-start(bf16[3,3,8,32,512]{4,3,1,0,2:T(8,128)(2,1)} %bitcast.27), calls=%async_computation | async-start | bytes 4718592 | tf_op jit(solution)/shard_map/all_to_all | solution.py:38
  18.4 135.2 %all-reduce.2.cloned.1.call-start = ((), (), s32[]{:S(2)}) async-start(), calls=%async_computation.3 | async-start | bytes 4718592 | tf_op jit(solution)/shard_map/psum | solution.py:9
  80.6 222.0 %reduce-scatter.3.cloned.1.call-start = ((), (), s32[]{:S(2)}) async-start(), calls=%async_computation.4 | async-start | bytes 14155776 | tf_op jit(solution)/shard_map/reduce_scatter | solution.py:40
  173.4 273.7 %reduce-scatter.5.cloned.1.call-start = ((), (), s32[]{:S(2)}) async-start(), calls=%async_computation.5 | async-start | bytes 3244032 | tf_op jit(solution)/shard_map/reduce_scatter | solution.py:48
  307.8 139.3 %copy-start.2 = (f32[3,16,512]{2,1,0:T(8,128)S(1)}, f32[3,16,512]{2,1,0:T(8,128)}, u32[]{:S(2)}) copy-start(f32[3,16,512]{2,1,0:T(8,128)} %param.7) | copy-start | bytes 294916
Sparse Core Ops, SparseCore 0:
  80.7 72.7 all-reduce.1
  173.5 129.1 reduce-scatter.2
  308.0 139.0 reduce-scatter.4
where the time goes:
time: 456 us; the launch traced here: 455 us
  waiting for transfers between devices  395 us (87%)
  local copies, waits for them, and re-layouts  19.7 us (4%)
  between operations  13.8 us (3%)
  matrix products  11.3 us (2%)
  other arithmetic  8.76 us (2%)
  starting transfers between devices  6.47 us (1%)
    reduce_scatter x1, waiting for transfers between devices, body(): lax.psum_scatter(partial_value, ('prow', 'pcol'), scatter_dimension=1, ti...  138 us
    reduce_scatter x1, waiting for transfers between devices, body(): lax.psum_scatter(local_product(anc_inverse, columns), 'pcol', scatter_dim...  129 us
    psum x1, waiting for transfers between devices, spread(): return lax.psum(jnp.where(mine, x, jnp.zeros_like(x)), axis)  72.9 us
    all_to_all x1, waiting for transfers between devices, body(): lax.all_to_all(outgoing, 'pcol', split_axis=2, concat_axis=3, tiled=True)  54.7 us
    transpose x1, local copies, waits for them, and re-layouts, local_product(): jnp.einsum('aibj,sbjw->isaw', anc_block, columns, preferred_element_type=...  11.9 us
  transfers between devices with their start and end apart: 4, of which 4 were waited for; matrix products, arithmetic and copies ran while one was open for 0% of the time, Pallas kernels for 0%

commit v1 on v0

--- a/solution.py
+++ b/solution.py
@@ -2,6 +2,12 @@
 import jax.numpy as jnp
 from jax import lax
 from jax.sharding import PartitionSpec as P
+
+
+def _switch_samples(w_in):
+    return jnp.concatenate(
+        lax.all_to_all(jnp.stack(jnp.split(w_in, lax.psum(1, "pcol"), 2), 0), "pcol", 0, 0), 3
+    )
 
 
 def spread(x, axis, root):
@@ -35,7 +41,7 @@
     masked = panel * keep
     outgoing = outbound(masked, n_row, n_col)
     root = col_pos % n_row
-    arrived = lax.all_to_all(outgoing, "pcol", split_axis=2, concat_axis=3, tiled=True)
+    arrived = _switch_samples(outgoing)
     columns = spread(arrived.reshape(sets, -1, tile_size, width), "prow", root)
     summed = lax.psum_scatter(
         local_product(anc_inverse, columns), "pcol", scatter_dimension=0, tiled=True

time: 456 us -> 461 us (1.011)
  local copies, waits for them, and re-layouts: 19.7 us -> 25.8 us
    unnamed x7 -> x14, local copies, waits for them, and re-layouts: 1.82 us -> 7.03 us
where the time goes in v1:
time: 461 us; the launch traced here: 460 us
  waiting for transfers between devices  395 us (86%)
  local copies, waits for them, and re-layouts  25.8 us (6%)
  between operations  13.8 us (3%)
  matrix products  11.3 us (2%)
  other arithmetic  7.36 us (2%)
  starting transfers between devices  6.47 us (1%)
    reduce_scatter x1, waiting for transfers between devices, body(): lax.psum_scatter(partial_value, ('prow', 'pcol'), scatter_dimension=1, ti...  139 us
    reduce_scatter x1, waiting for transfers between devices, body(): lax.psum_scatter(local_product(anc_inverse, columns), 'pcol', scatter_dim...  129 us
    psum x1, waiting for transfers between devices, spread(): return lax.psum(jnp.where(mine, x, jnp.zeros_like(x)), axis)  72.6 us
    all_to_all x1, waiting for transfers between devices, _switch_samples(): lax.all_to_all(jnp.stack(jnp.split(w_in, lax.psum(1, 'pcol'), 2), 0), 'pc...  54.7 us
    transpose x1, local copies, waits for them, and re-layouts, local_product(): jnp.einsum('aibj,sbjw->isaw', anc_block, columns, preferred_element_type=...  11.9 us
  transfers between devices with their start and end apart: 4, of which 4 were waited for; matrix products, arithmetic and copies ran while one was open for 0% of the time, Pallas kernels for 0%

profile of v1, /device:TPU:0, one launch (start us, length us, event | category | flops | bytes accessed | tf_op | source)
XLA Modules:
  0.0 460.2 jit_solution(8669992832942973123)
XLA Ops:
  7.2 0.0 copy-start
  7.2 0.1 fusion.14
  7.3 1.0 multiply_reduce_fusion
  8.2 1.2 broadcast_multiply_fusion
  9.4 0.0 copy-start.1
  9.4 0.8 copy-done.1
  10.3 0.3 broadcast_in_dim.4
  10.6 0.8 fusion.11
  11.3 0.7 fusion.10
  12.1 0.7 fusion.9
  12.8 0.7 fusion.8
  13.6 0.7 fusion.7
  14.3 0.8 fusion.6
  15.1 0.7 fusion.5
  15.8 0.8 fusion.4
  16.6 6.4 %all-to-all-start = ((bf16[8,3,3,1,32,512]{5,4,2,1,3,0:T(8,128)(2,1)}), bf16[8,3,3,1,32,512]{5,4,2,1,3,0:T(8,128)(2,1)}, u32[]{:S(2)}, u32[]{:S(2)}) async-start(bf16[8,3,3,1,32,512]{5,4,2,1,3,0:T(8,128)(2,1)} %fusion.4), calls=%async_computation | async-start | bytes 4718592 | tf_op jit(solution)/shard_map/all_to_all | solution.py:9
  22.9 0.0 all-reduce.2.cloned.1.call-start
  23.0 54.7 %all-to-all-done = bf16[8,3,3,1,32,512]{5,4,2,1,3,0:T(8,128)(2,1)} async-done(((bf16[8,3,3,1,32,512]{5,4,2,1,3,0:T(8,128)(2,1)}), bf16[8,3,3,1,32,512]{5,4,2,1,3,0:T(8,128)(2,1)}, u32[]{:S(2)}, u32[]{:S(2)}) %all-to-all-start) | async-done | bytes 2359328 | tf_op jit(solution)/shard_map/all_to_all | solution.py:9
  77.7 1.8 select_bitcast_fusion
  79.5 1.6 copy.28
  81.1 4.3 copy.29
  85.4 0.0 all-reduce.2.cloned.1.call-update
  85.4 0.0 reduce-scatter.3.cloned.1.call-start
  85.4 72.6 %all-reduce.2.cloned.1.call-done = bf16[3,3,256,512]{2,3,1,0:T(8,128)(2,1)} async-done(((bf16[3,3,256,512]{2,3,1,0:T(8,128)(2,1)}), bf16[3,3,256,512]{2,3,1,0:T(8,128)(2,1)}) %all-reduce.2.cloned.1.call-update) | async-done | bytes 2359312 | tf_op jit(solution)/shard_map/psum | solution.py:15
  158.0 0.0 copy-done
  158.0 7.9 %convolution_bitcast_fusion = f32[256,3,6,512]{0,3,2,1:T(8,128)} fusion(bf16[3,3,256,512]{2,3,1,0:T(8,128)(2,1)} %all-reduce.2.cloned.1.call-done, bf16[6,256,3,256]{3,1,2,0:T(8,128)(2,1)S(1)} %copy-done), kind=kOutput, calls=%fused_computation | convolution fusion | flops 3623878656 | bytes 14155776 | tf_op jit(solution)/shard_map/aibj,sbjw->isaw/dot_general | solution.py:19
  166.0 11.9 %copy.30 = f32[256,3,6,512]{3,2,1,0:T(8,128)} copy(f32[256,3,6,512]{0,3,2,1:T(8,128)} %convolution_bitcast_fusion) | data formatting | bytes 18874368 | tf_op jit(solution)/shard_map/aibj,sbjw->isaw/transpose | solution.py:19
  177.8 0.0 reduce-scatter.3.cloned.1.call-update
  177.8 0.0 reduce-scatter.5.cloned.1.call-start
  177.9 129.2 %reduce-scatter.3.cloned.1.call-done = f32[32,3,6,512]{3,2,1,0:T(8,128)} async-done(((f32[256,3,6,512]{3,2,1,0:T(8,128)}), f32[32,3,6,512]{3,2,1,0:T(8,128)}) %reduce-scatter.3.cloned.1.call-update) | async-done | bytes 1179664 | tf_op jit(solution)/shard_map/reduce_scatter | solution.py:46
  307.1 1.8 fusion.13
  308.9 3.4 convolution_bitcast_fusion.1
  312.3 0.0 copy-start.2
  312.3 0.0 reduce-scatter.5.cloned.1.call-update
  312.3 1.0 copy.32
  313.3 138.8 %reduce-scatter.5.cloned.1.call-done = f32[3,16,512]{2,1,0:T(8,128)} async-done(((f32[3,512,512]{2,1,0:T(8,128)}), f32[3,16,512]{2,1,0:T(8,128)}) %reduce-scatter.5.cloned.1.call-update) | async-done | bytes 98320 | tf_op jit(solution)/shard_map/reduce_scatter | solution.py:54
  452.1 0.0 copy-done.2
  452.1 1.5 sub.3
  (3 shorter events, 0.1 us)
Async XLA Ops:
  7.2 150.9 %copy-start = (bf16[6,256,3,256]{3,1,2,0:T(8,128)(2,1)S(1)}, bf16[6,256,3,256]{3,1,2,0:T(8,128)(2,1)}, u32[]{:S(2)}) copy-start(bf16[6,256,3,256]{3,1,2,0:T(8,128)(2,1)} %param.4) | copy-start | bytes 7077892
  9.4 0.8 copy-start.1
  16.6 61.1 %all-to-all-start = ((bf16[8,3,3,1,32,512]{5,4,2,1,3,0:T(8,128)(2,1)}), bf16[8,3,3,1,32,512]{5,4,2,1,3,0:T(8,128)(2,1)}, u32[]{:S(2)}, u32[]{:S(2)}) async-start(bf16[8,3,3,1,32,512]{5,4,2,1,3,0:T(8,128)(2,1)} %fusion.4), calls=%async_computation | async-start | bytes 4718592 | tf_op jit(solution)/shard_map/all_to_all | solution.py:9
  22.9 135.1 %all-reduce.2.cloned.1.call-start = ((), (), s32[]{:S(2)}) async-start(), calls=%async_computation.3 | async-start | bytes 4718592 | tf_op jit(solution)/shard_map/psum | solution.py:15
  85.4 221.7 %reduce-scatter.3.cloned.1.call-start = ((), (), s32[]{:S(2)}) async-start(), calls=%async_computation.4 | async-start | bytes 14155776 | tf_op jit(solution)/shard_map/reduce_scatter | solution.py:46
  177.8 274.2 %reduce-scatter.5.cloned.1.call-start = ((), (), s32[]{:S(2)}) async-start(), calls=%async_computation.5 | async-start | bytes 3244032 | tf_op jit(solution)/shard_map/reduce_scatter | solution.py:54
  312.3 139.8 %copy-start.2 = (f32[3,16,512]{2,1,0:T(8,128)S(1)}, f32[3,16,512]{2,1,0:T(8,128)}, u32[]{:S(2)}) copy-start(f32[3,16,512]{2,1,0:T(8,128)} %param.7) | copy-start | bytes 294916
Sparse Core Ops, SparseCore 0:
  85.5 72.4 all-reduce.1
  178.0 129.1 reduce-scatter.2
  312.4 139.6 reduce-scatter.4
